TPU v7x, 32 devices: a whole 2x2x4 slice. The times are simulated.
32 devices in a mesh: ctx: 8 (over y, x, core), ch: 4 (over z).
Axes of the slice: x: 2, y: 2, z: 4, core: 2. Of those that a mesh axis runs over, the one named last changes fastest.
Arguments:
- query_act: bfloat16 [4096, 4096], P('ctx', 'ch'), may hold values from -6 to 6
- key_act: bfloat16 [4096, 4096], P('ctx', 'ch'), may hold values from -6 to 6
- value_act: bfloat16 [4096, 4096], P('ctx', 'ch'), may hold values from -6 to 6
- filters: bfloat16 [4096, 128], P('ch'), may hold values from -0.5 to 0.5
- proj_weight: bfloat16 [8192, 4096], P('ctx', 'ch'), may hold values from -0.09375 to 0.09375
- cotangent: bfloat16 [4096, 8192], P('ctx', 'ch'), may hold values from -6 to 6
Outputs:
- grad_query: bfloat16 [4096, 4096], P('ctx', 'ch')
- grad_key: bfloat16 [4096, 4096], P('ctx', 'ch')
- grad_value: bfloat16 [4096, 4096], P('ctx', 'ch')
- grad_filter: float32 [4096, 128], P('ch')
- grad_proj: float32 [8192, 4096], P('ctx', 'ch')
All inputs are finite; a program needn't handle non-finite values.
Results may differ from a plain program's by a relative error of at most 0.0051.
Values may be sent and summed in bfloat16 or wider, within the bound.
A program may use at most 192 MiB of HBM per device.

v0:
```python
import jax
import jax.numpy as jnp
import numpy as np
from jax import lax
from jax.sharding import PartitionSpec as P

TAPS = 128


def from_behind(x, axis, by):
    length = lax.axis_size(axis)
    pairs = [(i, i + by) for i in range(length) if 0 <= i + by < length]
    return lax.ppermute(x, axis, pairs)


def basis(points):
    freqs = points // 2
    phase = (2 * np.arange(freqs)[:, None] + 1) * np.arange(points)[None, :] % (2 * points)
    angle = np.pi * phase / points
    return np.concatenate([np.cos(angle), np.sin(angle)], 0).astype(np.float32)


def split(a):
    a = jnp.asarray(a, jnp.float32)
    hi = a.astype(jnp.bfloat16)
    return (hi, (a - hi.astype(jnp.float32)).astype(jnp.bfloat16))


def dot32(a, b):
    return jnp.dot(a, b, preferred_element_type=jnp.float32)


def forward(table, x):
    hi, lo = split(table)
    return dot32(hi, x) + dot32(lo, x)


def backward(table, y):
    thi, tlo = split(table)
    yhi, ylo = split(y)
    return dot32(thi, yhi) + dot32(thi, ylo) + dot32(tlo, yhi)


def halves(x):
    n = x.shape[0] // 2
    return (x[:n], x[n:])


def times(x, f):
    (xc, xs), (fc, fs) = (halves(x), halves(f))
    return jnp.concatenate([xc * fc - xs * fs, xc * fs + xs * fc], 0)


def times_conj(x, f):
    (xc, xs), (fc, fs) = (halves(x), halves(f))
    return jnp.concatenate([xc * fc + xs * fs, xs * fc - xc * fs], 0)


def shards(query_act, key_act, value_act, filters, proj_weight, cotangent):
    tokens = query_act.shape[0]
    points = tokens + TAPS
    table = basis(points)
    inverse = (table.T / (points // 2)).astype(np.float32)
    gathered = lax.all_gather(cotangent, "ch", axis=1, tiled=True)
    weight = lax.all_gather(proj_weight, "ctx", axis=0, tiled=True)
    query_f = query_act.astype(jnp.float32)
    key_f = key_act.astype(jnp.float32)
    value_f = value_act.astype(jnp.float32)
    product = (key_f * value_f).astype(jnp.bfloat16)
    before = from_behind(product[tokens - TAPS :], "ctx", 1)
    filt_spec = forward(table[:, :TAPS], filters.T)
    prod_spec = forward(table[:, :TAPS], before) + forward(table[:, TAPS:], product)
    mixed = backward(inverse[TAPS:], times(prod_spec, filt_spec))
    gated = (query_f * mixed).astype(jnp.bfloat16)
    partial_grad = lax.dot_general(
        gathered, gated, (((0,), (0,)), ((), ())), preferred_element_type=jnp.float32
    ).astype(jnp.bfloat16)
    grad_proj = lax.psum_scatter(partial_grad, "ctx", scatter_dimension=0, tiled=True).astype(
        jnp.float32
    )
    grad_mix = dot32(gathered, weight)
    grad_query = (grad_mix * mixed).astype(jnp.bfloat16)
    grad_gate = (grad_mix * query_f).astype(jnp.bfloat16)
    after = from_behind(grad_gate[:TAPS], "ctx", -1)
    own_spec = forward(table[:, :tokens], grad_gate)
    gate_spec = own_spec + forward(table[:, tokens:], after)
    lags = inverse[TAPS - np.arange(TAPS)]
    local_filter = backward(lags, times_conj(prod_spec, own_spec))
    grad_filter = lax.psum(local_filter, "ctx").T
    grad_prod = backward(inverse[:tokens], times_conj(gate_spec, filt_spec))
    grad_key = (grad_prod * value_f).astype(jnp.bfloat16)
    grad_value = (grad_prod * key_f).astype(jnp.bfloat16)
    return (grad_query, grad_key, grad_value, grad_filter, grad_proj)


def solution(mesh):
    return jax.shard_map(
        shards,
        mesh=mesh,
        in_specs=(
            P("ctx", "ch"),
            P("ctx", "ch"),
            P("ctx", "ch"),
            P("ch", None),
            P("ctx", "ch"),
            P("ctx", "ch"),
        ),
        out_specs=(P("ctx", "ch"), P("ctx", "ch"), P("ctx", "ch"), P("ch", None), P("ctx", "ch")),
        check_vma=False,
    )
```

profile of v0, /device:TPU:0, one launch (start us, length us, event | category | flops | bytes accessed | tf_op | source)
XLA Modules:
  0.0 497.0 jit_solution(8108205557831197759)
XLA Ops:
  8.8 1.3 copy.19
  10.1 1.3 copy.20
  12.4 149.5 %all-gather.3.cloned.1.call-done = bf16[512,8192]{1,0:T(8,128)(2,1)} async-done(((bf16[512,2048]{1,0:T(8,128)(2,1)}), bf16[512,8192]{1,0:T(8,128)(2,1)}) %all-gather.3.cloned.1.call-update) | async-done | bytes 8388624 | tf_op jit(solution)/shard_map/all_gather | solution.py:64
  162.0 90.0 %all-gather.5.cloned.1.call-done = bf16[8192,1024]{1,0:T(8,128)(2,1)} async-done(((bf16[1024,1024]{1,0:T(8,128)(2,1)}), bf16[8192,1024]{1,0:T(8,128)(2,1)}) %all-gather.5.cloned.1.call-update) | async-done | bytes 16777232 | tf_op jit(solution)/shard_map/all_gather | solution.py:65
  251.9 14.9 %fusion.6 = (bf16[512,1024]{1,0:T(8,128)(2,1)S(1)}, f32[512,1024]{1,0:T(8,128)S(1)}) fusion(bf16[512,1024]{1,0:T(8,128)(2,1)} %param.14, bf16[512,8192]{1,0:T(8,128)(2,1)} %all-gather.3.cloned.1.call-done, bf16[8192,1024]{1,0:T(8,128)(2,1)} %all-gather.5.cloned.1.call-done), kind=kOutput, calls=%fused_computation.20 | convolution fusion | flops 8591507456 | bytes 29360128 | tf_op jit(solution)/shard_map/dot_general | solution.py:30
  266.9 1.4 collective-permute-start.1
  272.6 1.0 fusion.8
  273.7 1.0 fusion.21
  275.4 2.7 fusion.3
  278.1 6.7 %collective-permute-start = (bf16[128,1024]{0,1:T(8,128)(2,1)S(1)}, bf16[128,1024]{0,1:T(8,128)(2,1)S(1)}, u32[]{:S(2)}, u32[]{:S(2)}) collective-permute-start(bf16[128,1024]{0,1:T(8,128)(2,1)S(1)} %slice.44), channel_id=1, source_target_pairs={{0,4},{4,8},{8,12},{12,16},{16,20},{20,24},{24,28},{1,5},{5,9},{9,... | collective-permute-start | bytes 786440 | tf_op jit(solution)/shard_map/ppermute | solution.py:13
  285.7 0.9 fusion.37
  288.2 2.5 multiply_add_fusion
  290.7 1.0 fusion.14
  291.8 1.0 fusion.17
  292.8 2.1 multiply_convert_fusion
  294.9 15.9 %convert_bitcast_fusion = bf16[8192,1024]{0,1:T(8,128)(2,1)} fusion(bf16[512,8192]{1,0:T(8,128)(2,1)} %all-gather.3.cloned.1.call-done, f32[512,1024]{1,0:T(8,128)S(1)} %get-tuple-element.24, bf16[512,1024]{1,0:T(8,128)(2,1)S(1)} %copy-done.25), kind=kOutput, calls=%fused_computation | convolution fusion | flops 8599896064 | bytes 28311552 | tf_op jit(solution)/shard_map/dot_general | solution.py:75
  311.0 1.0 copy-done.2
  313.9 1.4 fusion.12
  315.4 2.4 copy.26
  317.7 1.3 copy.25
  319.0 111.5 %reduce-scatter.2.cloned.1.call-done = bf16[1024,1024]{0,1:T(8,128)(2,1)} async-done(((bf16[8192,1024]{0,1:T(8,128)(2,1)}), bf16[1024,1024]{0,1:T(8,128)(2,1)}) %reduce-scatter.2.cloned.1.call-update) | async-done | bytes 2097168 | tf_op jit(solution)/shard_map/reduce_scatter | solution.py:78
  430.5 4.2 copy.27
  434.6 53.9 %all-reduce.2.cloned.1.call-done = f32[1024,128]{1,0:T(8,128)} async-done(((f32[1024,128]{1,0:T(8,128)}), f32[1024,128]{1,0:T(8,128)}) %all-reduce.2.cloned.1.call-update) | async-done | bytes 524304 | tf_op jit(solution)/shard_map/psum | solution.py:89
  488.6 1.9 copy.33
  (75 shorter events, 12.2 us)
Async XLA Ops:
  7.2 4.2 copy-start
  7.2 1.6 copy-start.10
  7.2 154.8 %all-gather.3.cloned.1.call-start = ((), (), s32[]{:S(2)}) async-start(), calls=%async_computation.1 | async-start | bytes 10485760 | tf_op jit(solution)/shard_map/all_gather | solution.py:64
  7.9 2.2 copy-start.11
  7.9 244.0 %all-gather.5.cloned.1.call-start = ((), (), s32[]{:S(2)}) async-start(), calls=%async_computation.2 | async-start | bytes 18874368 | tf_op jit(solution)/shard_map/all_gather | solution.py:65
  8.7 2.7 copy-start.20
  8.7 421.8 %reduce-scatter.2.cloned.1.call-start = ((), (), s32[]{:S(2)}) async-start(), calls=%async_computation.4 | async-start | bytes 18874368 | tf_op jit(solution)/shard_map/reduce_scatter | solution.py:78
  10.1 1.8 copy-start.13
  12.4 255.9 %copy-start.9 = (bf16[640,512]{1,0:T(8,128)(2,1)S(1)}, bf16[640,512]{1,0:T(8,128)(2,1)}, u32[]{:S(2)}) copy-start(bf16[640,512]{1,0:T(8,128)(2,1)} %constant.33) | copy-start | bytes 1966084
  266.9 2.3 copy-start.18
  266.9 3.6 collective-permute-start.1
  273.7 1.5 copy-start.6
  273.7 1.7 copy-start.12
  275.4 9.4 %copy-start.17 = (bf16[640,512]{1,0:T(8,128)(2,1)S(1)}, bf16[640,512]{1,0:T(8,128)(2,1)}, u32[]{:S(2)}) copy-start(bf16[640,512]{1,0:T(8,128)(2,1)} %constant.28) | copy-start | bytes 1966084
  278.1 7.6 %copy-start.16 = (bf16[640,512]{1,0:T(8,128)(2,1)S(1)}, bf16[640,512]{1,0:T(8,128)(2,1)}, u32[]{:S(2)}) copy-start(bf16[640,512]{1,0:T(8,128)(2,1)} %constant.25) | copy-start | bytes 1966084
  278.1 8.5 %collective-permute-start = (bf16[128,1024]{0,1:T(8,128)(2,1)S(1)}, bf16[128,1024]{0,1:T(8,128)(2,1)S(1)}, u32[]{:S(2)}, u32[]{:S(2)}) collective-permute-start(bf16[128,1024]{0,1:T(8,128)(2,1)S(1)} %slice.44), channel_id=1, source_target_pairs={{0,4},{4,8},{8,12},{12,16},{16,20},{20,24},{24,28},{1,5},{5,9},{9,... | collective-permute-start | bytes 786440 | tf_op jit(solution)/shard_map/ppermute | solution.py:13
  288.2 2.5 copy-start.15
  292.7 2.1 copy-start.25
  310.7 1.3 copy-start.2
  310.7 1.7 copy-start.3
  310.7 1.7 copy-start.19
  310.8 177.8 %all-reduce.2.cloned.1.call-start = ((), (), s32[]{:S(2)}) async-start(), calls=%async_computation.3 | async-start | bytes 1048576 | tf_op jit(solution)/shard_map/psum | solution.py:89
  315.3 2.4 copy-start.4
  430.5 60.0 %copy-start.1 = (bf16[1024,128]{1,0:T(8,128)(2,1)S(1)}, bf16[1024,128]{1,0:T(8,128)(2,1)}, u32[]{:S(2)}) copy-start(bf16[1024,128]{1,0:T(8,128)(2,1)} %param.17) | copy-start | bytes 786436
  (8 other events, 8.3 us)
Sparse Core Ops, SparseCore 0:
  9.6 152.3 all-gather.2
  163.9 88.0 all-gather.4
  310.9 119.5 reduce-scatter.1
  434.0 54.5 all-reduce.1
where the time goes:
time: 498 us; the launch traced here: 497 us
  waiting for transfers between devices  407 us (82%)
  matrix products  48.7 us (10%)
  local copies, waits for them, and re-layouts  15.9 us (3%)
  between operations  14.1 us (3%)
  starting transfers between devices  8.5 us (2%)
    all_gather x1, waiting for transfers between devices, shards(): gathered = lax.all_gather(cotangent, 'ch', axis=1, tiled=True)  150 us
    reduce_scatter x1, waiting for transfers between devices, shards(): lax.psum_scatter(partial_grad, 'ctx', scatter_dimension=0, tiled=True)  111 us
    all_gather x1, waiting for transfers between devices, shards(): weight = lax.all_gather(proj_weight, 'ctx', axis=0, tiled=True)  90 us
    psum x1, waiting for transfers between devices, shards(): grad_filter = lax.psum(local_filter, 'ctx').T  53.9 us
    dot_general x20, matrix products, dot32(): return jnp.dot(a, b, preferred_element_type=jnp.float32)  32.9 us
    dot_general x1, matrix products, shards(): lax.dot_general(gathered, gated, (((0,), (0,)), ((), ())), preferred_elem...  15.9 us
    unnamed x58, local copies, waits for them, and re-layouts  15.9 us
  transfers between devices with their start and end apart: 6, of which 5 were waited for; matrix products, arithmetic and copies ran while one was open for 4% of the time, Pallas kernels for 0%

commit v1 on v0

--- a/solution.py
+++ b/solution.py
@@ -86,7 +86,7 @@
     gate_spec = own_spec + forward(table[:, tokens:], after)
     lags = inverse[TAPS - np.arange(TAPS)]
     local_filter = backward(lags, times_conj(prod_spec, own_spec))
-    grad_filter = lax.psum(local_filter, "ctx").T
+    grad_filter = jnp.sum(lax.all_gather(local_filter, "ctx"), axis=0).T
     grad_prod = backward(inverse[:tokens], times_conj(gate_spec, filt_spec))
     grad_key = (grad_prod * value_f).astype(jnp.bfloat16)
     grad_value = (grad_prod * key_f).astype(jnp.bfloat16)

time: 498 us -> 466 us (0.936)
  waiting for transfers between devices: 407 us -> 372 us
    psum x1 -> x0, waiting for transfers between devices: 53.9 us -> none  [shards(): grad_filter = lax.psum(local_filter, 'ctx').T]
    all_gather x0 -> x1, waiting for transfers between devices: none -> 16.2 us  [shards(): grad_filter = jnp.sum(lax.all_gather(local_filter, 'ctx'), axis=0).T]
    unnamed x58 -> x62, local copies, waits for them, and re-layouts: 15.9 us -> 17 us
  transfers between devices with their start and end apart: 6 -> 6, of which waited for: 5 -> 5; matrix products, arithmetic and copies ran while one was open for 4% -> 7% of each run, Pallas kernels for 0% -> 0%
where the time goes in v1:
time: 466 us
  waiting for transfers between devices  372 us (80%)
  matrix products  49.7 us (11%)
  local copies, waits for them, and re-layouts  17.1 us (4%)
  between operations  14.1 us (3%)
  starting transfers between devices  8.28 us (2%)
  other arithmetic  4.82 us (1%)
    all_gather x1, waiting for transfers between devices, shards(): gathered = lax.all_gather(cotangent, 'ch', axis=1, tiled=True)  150 us
    reduce_scatter x1, waiting for transfers between devices, shards(): lax.psum_scatter(partial_grad, 'ctx', scatter_dimension=0, tiled=True)  114 us
    all_gather x1, waiting for transfers between devices, shards(): weight = lax.all_gather(proj_weight, 'ctx', axis=0, tiled=True)  90 us
    dot_general x20, matrix products, dot32(): return jnp.dot(a, b, preferred_element_type=jnp.float32)  33.8 us
    unnamed x62, local copies, waits for them, and re-layouts  17 us
    all_gather x1, waiting for transfers between devices, shards(): grad_filter = jnp.sum(lax.all_gather(local_filter, 'ctx'), axis=0).T  16.2 us
    dot_general x1, matrix products, shards(): lax.dot_general(gathered, gated, (((0,), (0,)), ((), ())), preferred_elem...  15.9 us
  transfers between devices with their start and end apart: 6, of which 5 were waited for; matrix products, arithmetic and copies ran while one was open for 7% of the time, Pallas kernels for 0%

profile of v1, /device:TPU:0, one launch (start us, length us, event | category | flops | bytes accessed | tf_op | source)
XLA Modules:
  0.0 465.9 jit_solution(12721726044679813946)
XLA Ops:
  8.8 1.3 copy.19
  10.1 1.3 copy.20
  12.4 149.5 %all-gather.5.cloned.1.call-done = bf16[512,8192]{1,0:T(8,128)(2,1)} async-done(((bf16[512,2048]{1,0:T(8,128)(2,1)}), bf16[512,8192]{1,0:T(8,128)(2,1)}) %all-gather.5.cloned.1.call-update) | async-done | bytes 8388624 | tf_op jit(solution)/shard_map/all_gather | solution.py:64
  162.0 90.0 %all-gather.7.cloned.1.call-done = bf16[8192,1024]{1,0:T(8,128)(2,1)} async-done(((bf16[1024,1024]{1,0:T(8,128)(2,1)}), bf16[8192,1024]{1,0:T(8,128)(2,1)}) %all-gather.7.cloned.1.call-update) | async-done | bytes 16777232 | tf_op jit(solution)/shard_map/all_gather | solution.py:65
  251.9 15.9 %fusion.6 = (bf16[512,1024]{1,0:T(8,128)(2,1)S(1)}, f32[512,1024]{1,0:T(8,128)}) fusion(bf16[512,1024]{1,0:T(8,128)(2,1)} %param.14, bf16[512,8192]{1,0:T(8,128)(2,1)} %all-gather.5.cloned.1.call-done, bf16[8192,1024]{1,0:T(8,128)(2,1)} %all-gather.7.cloned.1.call-done), kind=kOutput, calls=%fused_computation.21 | convolution fusion | flops 8591507456 | bytes 29360128 | tf_op jit(solution)/shard_map/dot_general | solution.py:30
  267.8 1.4 collective-permute-start.1
  273.6 1.0 fusion.8
  274.7 1.0 fusion.20
  276.4 2.7 fusion.3
  279.1 6.7 %collective-permute-start = (bf16[128,1024]{0,1:T(8,128)(2,1)S(1)}, bf16[128,1024]{0,1:T(8,128)(2,1)S(1)}, u32[]{:S(2)}, u32[]{:S(2)}) collective-permute-start(bf16[128,1024]{0,1:T(8,128)(2,1)S(1)} %slice.44), channel_id=1, source_target_pairs={{0,4},{4,8},{8,12},{12,16},{16,20},{20,24},{24,28},{1,5},{5,9},{9,... | collective-permute-start | bytes 786440 | tf_op jit(solution)/shard_map/ppermute | solution.py:13
  289.2 2.4 multiply_add_fusion
  293.1 1.4 convolution_add_fusion.2
  295.2 1.0 fusion.13
  296.2 1.0 fusion.16
  297.8 2.0 multiply_convert_fusion
  299.9 15.9 %convert_bitcast_fusion = bf16[8192,1024]{0,1:T(8,128)(2,1)} fusion(bf16[512,8192]{1,0:T(8,128)(2,1)} %all-gather.5.cloned.1.call-done, f32[512,1024]{1,0:T(8,128)S(1)} %get-tuple-element.24, bf16[512,1024]{1,0:T(8,128)(2,1)S(1)} %copy-done.27), kind=kOutput, calls=%fused_computation | convolution fusion | flops 8599896064 | bytes 28311552 | tf_op jit(solution)/shard_map/dot_general | solution.py:75
  315.8 1.2 copy-done.5
  317.0 1.3 copy.26
  318.3 1.3 copy.25
  319.6 16.2 %all-gather.9.cloned.1.call-done = f32[1024,1024]{0,1:T(8,128)} async-done(((f32[128,1024]{0,1:T(8,128)}), f32[1024,1024]{0,1:T(8,128)}) %all-gather.9.cloned.1.call-update) | async-done | bytes 4194320 | tf_op jit(solution)/shard_map/all_gather | solution.py:89
  335.8 3.2 copy.32
  339.0 1.8 bitcast_reduce_fusion
  340.8 114.4 %reduce-scatter.2.cloned.1.call-done = bf16[1024,1024]{0,1:T(8,128)(2,1)} async-done(((bf16[8192,1024]{0,1:T(8,128)(2,1)}), bf16[1024,1024]{0,1:T(8,128)(2,1)}) %reduce-scatter.2.cloned.1.call-update) | async-done | bytes 2097168 | tf_op jit(solution)/shard_map/reduce_scatter | solution.py:78
  455.2 4.1 copy.27
  (80 shorter events, 13.6 us)
Async XLA Ops:
  7.2 4.2 copy-start
  7.2 1.6 copy-start.12
  7.2 154.8 %all-gather.5.cloned.1.call-start = ((), (), s32[]{:S(2)}) async-start(), calls=%async_computation.1 | async-start | bytes 10485760 | tf_op jit(solution)/shard_map/all_gather | solution.py:64
  7.9 2.2 copy-start.13
  7.9 244.0 %all-gather.7.cloned.1.call-start = ((), (), s32[]{:S(2)}) async-start(), calls=%async_computation.2 | async-start | bytes 18874368 | tf_op jit(solution)/shard_map/all_gather | solution.py:65
  8.7 2.7 copy-start.21
  8.7 327.1 %all-gather.9.cloned.1.call-start = ((), (), s32[]{:S(2)}) async-start(), calls=%async_computation.4 | async-start | bytes 4718592 | tf_op jit(solution)/shard_map/all_gather | solution.py:89
  10.1 1.8 copy-start.15
  12.4 256.9 %copy-start.11 = (bf16[640,512]{1,0:T(8,128)(2,1)S(1)}, bf16[640,512]{1,0:T(8,128)(2,1)}, u32[]{:S(2)}) copy-start(bf16[640,512]{1,0:T(8,128)(2,1)} %constant.35) | copy-start | bytes 1966084
  267.8 2.3 copy-start.20
  267.8 3.6 collective-permute-start.1
  274.6 1.5 copy-start.7
  274.7 1.7 copy-start.14
  276.4 9.5 %copy-start.19 = (bf16[640,512]{1,0:T(8,128)(2,1)S(1)}, bf16[640,512]{1,0:T(8,128)(2,1)}, u32[]{:S(2)}) copy-start(bf16[640,512]{1,0:T(8,128)(2,1)} %constant.30) | copy-start | bytes 1966084
  279.1 7.6 %copy-start.18 = (bf16[640,512]{1,0:T(8,128)(2,1)S(1)}, bf16[640,512]{1,0:T(8,128)(2,1)}, u32[]{:S(2)}) copy-start(bf16[640,512]{1,0:T(8,128)(2,1)} %constant.27) | copy-start | bytes 1966084
  279.1 8.5 %collective-permute-start = (bf16[128,1024]{0,1:T(8,128)(2,1)S(1)}, bf16[128,1024]{0,1:T(8,128)(2,1)S(1)}, u32[]{:S(2)}, u32[]{:S(2)}) collective-permute-start(bf16[128,1024]{0,1:T(8,128)(2,1)S(1)} %slice.44), channel_id=1, source_target_pairs={{0,4},{4,8},{8,12},{12,16},{16,20},{20,24},{24,28},{1,5},{5,9},{9,... | collective-permute-start | bytes 786440 | tf_op jit(solution)/shard_map/ppermute | solution.py:13
  289.2 2.4 copy-start.23
  293.1 1.9 copy-start.3
  293.1 2.1 copy-start.17
  294.6 160.7 %reduce-scatter.2.cloned.1.call-start = ((), (), s32[]{:S(2)}) async-start(), calls=%async_computation.3 | async-start | bytes 18874368 | tf_op jit(solution)/shard_map/reduce_scatter | solution.py:78
  296.2 1.6 copy-start.10
  297.8 2.1 copy-start.27
  315.8 2.5 copy-start.4
  339.0 120.4 %copy-start.1 = (bf16[1024,128]{1,0:T(8,128)(2,1)S(1)}, bf16[1024,128]{1,0:T(8,128)(2,1)}, u32[]{:S(2)}) copy-start(bf16[1024,128]{1,0:T(8,128)(2,1)} %param.17) | copy-start | bytes 786436
  (10 other events, 11.1 us)
Sparse Core Ops, SparseCore 0:
  9.6 152.3 all-gather.4
  163.9 88.0 all-gather.6
  294.7 41.0 all-gather.8
  339.2 115.9 reduce-scatter.1
